TPU v7x, 256 devices: a whole 4x4x8 slice. The times are simulated.
256 devices in a mesh: shot: 16 (over x_lo, z), rcv: 8 (over y, x_hi), surf: 2 (over core).
Axes of the slice: x: 4 (x_hi: 2, x_lo: 2; x = x_hi * 2 + x_lo), y: 4, z: 8, core: 2. Of those that a mesh axis runs over, the one named last changes fastest.
Arguments:
- traces: bfloat16 [2, 16384, 256], P('surf', 'shot'), may hold values from -6 to 6
- trace_block: int32 [2, 16384, 1], P('surf', 'shot'), may hold values from 0 to 15; in each aligned block of 128 rows (0 to 127, 128 to 255, ..., all dimensions but the last counted through in order) at most 16 rows name the same one
- trace_shot: int32 [2, 16384], P('surf', 'shot'), may hold values from 0 to 15
- trace_point: int32 [2, 16384], P('surf', 'shot'), may hold values from 0 to 255
- recv_panel: bfloat16 [129, 2, 512, 1024], P(None, None, ('shot', 'surf'), 'rcv'), may hold values from -0.375 to 0.375
Outputs:
- multiples: bfloat16 [129, 2, 256, 1024], P(None, None, ('shot', 'surf'), 'rcv')
Inputs may be any that keep to these rules, and one draw needn't show every extreme that they name: `trace_block`: in each aligned block of 128 rows, at most 16 rows name one shot block.
All inputs are finite; a program needn't handle non-finite values.
Results may differ from a plain program's by a relative error of at most 0.012.
Values may be sent and summed in bfloat16 or wider, within the bound.
A program may use at most 64 MiB of HBM per device.

v0:
```python
import math

import jax
import jax.numpy as jnp
from jax import lax
from jax.sharding import PartitionSpec as P

SHOTS_PER_INDEX = 16


def split_up(array, dim, size):
    before, after = (array.shape[:dim], array.shape[dim + 1 :])
    return jnp.moveaxis(array.reshape(*before, size, -1, *after), dim, 0)


def summed_on_arrival(array, axis, dim):
    size = lax.axis_size(axis)
    parts = lax.all_to_all(split_up(array, dim, size), axis, 0, 0, tiled=True)
    return jnp.sum(parts.astype(jnp.float32), axis=0)


def transform_rows(samples, window_len, bin_count):
    sample_index = lax.broadcasted_iota(jnp.int32, (window_len, bin_count), 0)
    freq_index = lax.broadcasted_iota(jnp.int32, (window_len, bin_count), 1)
    phase_angle = (sample_index * freq_index % window_len).astype(jnp.float32) * (
        2.0 * math.pi / window_len
    )
    norm_factor = 1.0 / math.sqrt(window_len)
    table = jnp.concatenate(
        [jnp.cos(phase_angle) * norm_factor, -jnp.sin(phase_angle) * norm_factor], axis=1
    )
    table_high = table.astype(jnp.bfloat16)
    table_low = (table - table_high.astype(jnp.float32)).astype(jnp.bfloat16)
    result = jnp.dot(samples, table_high, preferred_element_type=jnp.float32)
    result = result + jnp.dot(samples, table_low, preferred_element_type=jnp.float32)
    real_part = result[:, :bin_count]
    imag_part = result[:, bin_count:]
    return jnp.stack([real_part, imag_part], axis=1).astype(jnp.bfloat16)


def route_rows(spectra, owners, targets, places, owner_count, empty_id):
    row_count = owners.shape[0]
    owner_hit = owners[:, None] == lax.broadcasted_iota(jnp.int32, (1, owner_count), 1)
    earlier = lax.broadcasted_iota(jnp.int32, (row_count, row_count), 0) > lax.broadcasted_iota(
        jnp.int32, (row_count, row_count), 1
    )
    before = jnp.dot(
        earlier.astype(jnp.bfloat16),
        owner_hit.astype(jnp.bfloat16),
        preferred_element_type=jnp.float32,
    )
    slot_rank = jnp.sum(jnp.where(owner_hit, before, 0.0), axis=1).astype(jnp.int32)
    position = owners * places + slot_rank
    slot_total = owner_count * places
    slot_hit = position[:, None] == lax.broadcasted_iota(jnp.int32, (1, slot_total), 1)
    flat_spectra = spectra.reshape(row_count, -1)
    buffer = lax.dot_general(
        slot_hit.astype(jnp.bfloat16),
        flat_spectra,
        (((0,), (0,)), ((), ())),
        preferred_element_type=jnp.float32,
    )
    buffer = buffer.astype(spectra.dtype)
    labels = jnp.max(jnp.where(slot_hit, targets[:, None], -1), axis=0)
    labels = jnp.where(labels < 0, empty_id, labels)
    return (
        buffer.reshape((owner_count, places) + spectra.shape[1:]),
        labels.reshape(owner_count, places),
    )


def bin_panel(received, labels, shot_rows, point_count):
    freq_count = received.shape[-1]
    flat_rows = received.reshape(-1, 2 * freq_count)
    flat_labels = labels.reshape(-1)
    point_iota = lax.broadcasted_iota(jnp.int32, (1, point_count), 1)

    def one_shot(shot_id):
        local_label = flat_labels - shot_id * point_count
        point_hit = local_label[:, None] == point_iota
        totals = lax.dot_general(
            point_hit.astype(jnp.bfloat16),
            flat_rows,
            (((0,), (0,)), ((), ())),
            preferred_element_type=jnp.float32,
        )
        coverage = jnp.sum(point_hit.astype(jnp.float32), axis=0)
        return (totals / jnp.maximum(coverage, 1.0)[:, None]).astype(jnp.bfloat16)

    panel = lax.map(one_shot, jnp.arange(shot_rows, dtype=jnp.int32))
    return panel.reshape(shot_rows, point_count, 2, freq_count).transpose(3, 2, 0, 1)


def product(left_edge, right_edge):
    return jnp.einsum("bhv,bvy->bhy", left_edge, right_edge, preferred_element_type=jnp.float32)


def local(traces, trace_block, trace_shot, trace_point, recv_panel):
    shot_count = lax.axis_size("shot")
    rcv_count = lax.axis_size("rcv")
    freq_count = recv_panel.shape[0]
    half_points = recv_panel.shape[2] * shot_count
    window_len = traces.shape[2]
    row_count = traces.shape[1]
    part_rows = row_count // rcv_count
    capacity = 2 * part_rows // shot_count
    empty_id = SHOTS_PER_INDEX * half_points
    samples = traces[0]
    owners = trace_block[0, :, 0]
    targets = trace_shot[0] * half_points + trace_point[0]
    spectra = transform_rows(samples, window_len, freq_count)
    buffer, labels = route_rows(
        spectra, owners, targets, rcv_count * capacity, shot_count, empty_id
    )
    received, got_labels = (
        lax.all_to_all(buffer, "shot", split_axis=0, concat_axis=0, tiled=True),
        lax.all_to_all(labels, "shot", split_axis=0, concat_axis=0, tiled=True),
    )
    panel = bin_panel(received, got_labels, SHOTS_PER_INDEX, half_points)
    receiver = lax.all_gather(recv_panel, "shot", axis=2, tiled=True)
    real_part = product(panel[:, 0], receiver[:, 0]) - product(panel[:, 1], receiver[:, 1])
    imag_part = product(panel[:, 0], receiver[:, 1]) + product(panel[:, 1], receiver[:, 0])
    partial_value = jnp.stack([real_part, imag_part], axis=1)
    half_term = lax.optimization_barrier(partial_value.astype(jnp.bfloat16)).astype(jnp.float32)
    result = summed_on_arrival(half_term.astype(jnp.bfloat16), "surf", 2)
    return result.astype(jnp.bfloat16)


def solution(mesh):
    in_specs = (
        P("surf", "shot", None),
        P("surf", "shot", None),
        P("surf", "shot"),
        P("surf", "shot"),
        P(None, None, ("shot", "surf"), "rcv"),
    )
    out_specs = P(None, None, ("shot", "surf"), "rcv")
    return jax.shard_map(local, mesh=mesh, in_specs=in_specs, out_specs=out_specs, check_vma=False)
```

profile of v0, /device:TPU:1, one launch (start us, length us, event | category | flops | bytes accessed | tf_op | source)
XLA Modules:
  0.0 263.0 jit_solution(1235971979130966523)
XLA Ops:
  6.5 2.4 copy.40
  11.5 1.8 fusion.17
  13.7 1.8 copy.36
  15.5 10.0 %all-to-all-start.1 = ((bf16[16,128,2,129]{1,2,3,0:T(2,128)(2,1)}), bf16[16,128,2,129]{1,2,3,0:T(2,128)(2,1)S(1)}, u32[]{:S(2)}, u32[]{:S(2)}) async-start(bf16[16,128,2,129]{1,2,3,0:T(2,128)(2,1)} %copy.36), calls=%async_computation.1 | async-start | bytes 2113536 | tf_op jit(solution)/shard_map/all_to_all | solution.py:116
  25.6 1.6 select_reduce_fusion
  27.9 34.8 %all-to-all-done.1 = bf16[16,128,2,129]{1,2,3,0:T(2,128)(2,1)S(1)} async-done(((bf16[16,128,2,129]{1,2,3,0:T(2,128)(2,1)}), bf16[16,128,2,129]{1,2,3,0:T(2,128)(2,1)S(1)}, u32[]{:S(2)}, u32[]{:S(2)}) %all-to-all-start.1) | async-done | bytes 1056800 | tf_op jit(solution)/shard_map/all_to_all | solution.py:116
  62.6 4.4 %all-to-all-start = ((s32[16,1,128]{2,1,0:T(1,128)}), s32[16,1,128]{2,1,0:T(1,128)S(1)}, u32[]{:S(2)}, u32[]{:S(2)}) async-start(s32[16,1,128]{2,1,0:T(1,128)} %compare_select_fusion), calls=%async_computation | async-start | bytes 16384 | tf_op jit(solution)/shard_map/all_to_all | solution.py:117
  67.0 8.1 %copy.44 = bf16[16,128,2,129]{3,2,1,0:T(2,128)(2,1)S(1)} copy(bf16[16,128,2,129]{1,2,3,0:T(2,128)(2,1)} %copy-done.2) | data formatting | bytes 2113536
  75.1 2.0 reshape.78
  77.1 74.6 %while.11 = (s32[]{:T(128)}, bf16[16,256,258]{1,2,0:T(8,128)(2,1)}, s32[16]{0:T(128)S(1)}, s32[2048]{0:T(1024)S(1)}, bf16[2048,258]{1,0:T(8,128)(2,1)}, /*index=5*/s32[]{:T(128)}, s32[1]{0:T(128)}) while((s32[]{:T(128)}, bf16[16,256,258]{1,2,0:T(8,128)(2,1)}, s32[16]{0:T(128)S(1)}, s32[2048]{0:T(1024)S(1)}, ...), condition=%wide.region_4.5_spmd.clone, body=%wide.region_2.4_spmd.clone.sunk | while | flops 272763904 | bytes 1745513 | solution.py:90
  78.7 3.1 %fusion.50 = bf16[16,256,258]{1,2,0:T(8,128)(2,1)} fusion(bf16[16,256,258]{1,2,0:T(8,128)(2,1)} %get-tuple-element.128, s32[]{:T(128)} %get-tuple-element.127, bf16[2048,258]{1,0:T(8,128)(2,1)} %get-tuple-element.138, s32[2048]{0:T(1024)S(1)} %broadcast_subtract_fusion.2, f32[256]{0:T(256)S(1)} %broadcast_maximum_fusion.2), kind=kOutput, calls=%fused_computation.8.clone.1 | convolution fusion | flops 271188992 | bytes 1717760 | tf_op jit(solution)/shard_map/while/body/eval_jaxpr/dot_general | solution.py:81
  83.4 3.0 %fusion.50 = bf16[16,256,258]{1,2,0:T(8,128)(2,1)} fusion(bf16[16,256,258]{1,2,0:T(8,128)(2,1)} %get-tuple-element.128, s32[]{:T(128)} %get-tuple-element.127, bf16[2048,258]{1,0:T(8,128)(2,1)} %get-tuple-element.138, s32[2048]{0:T(1024)S(1)} %broadcast_subtract_fusion.2, f32[256]{0:T(256)S(1)} %broadcast_maximum_fusion.2), kind=kOutput, calls=%fused_computation.8.clone.1 | convolution fusion | flops 271188992 | bytes 1717760 | tf_op jit(solution)/shard_map/while/body/eval_jaxpr/dot_general | solution.py:81
  88.1 3.1 %fusion.50 = bf16[16,256,258]{1,2,0:T(8,128)(2,1)} fusion(bf16[16,256,258]{1,2,0:T(8,128)(2,1)} %get-tuple-element.128, s32[]{:T(128)} %get-tuple-element.127, bf16[2048,258]{1,0:T(8,128)(2,1)} %get-tuple-element.138, s32[2048]{0:T(1024)S(1)} %broadcast_subtract_fusion.2, f32[256]{0:T(256)S(1)} %broadcast_maximum_fusion.2), kind=kOutput, calls=%fused_computation.8.clone.1 | convolution fusion | flops 271188992 | bytes 1717760 | tf_op jit(solution)/shard_map/while/body/eval_jaxpr/dot_general | solution.py:81
  92.7 3.0 %fusion.50 = bf16[16,256,258]{1,2,0:T(8,128)(2,1)} fusion(bf16[16,256,258]{1,2,0:T(8,128)(2,1)} %get-tuple-element.128, s32[]{:T(128)} %get-tuple-element.127, bf16[2048,258]{1,0:T(8,128)(2,1)} %get-tuple-element.138, s32[2048]{0:T(1024)S(1)} %broadcast_subtract_fusion.2, f32[256]{0:T(256)S(1)} %broadcast_maximum_fusion.2), kind=kOutput, calls=%fused_computation.8.clone.1 | convolution fusion | flops 271188992 | bytes 1717760 | tf_op jit(solution)/shard_map/while/body/eval_jaxpr/dot_general | solution.py:81
  97.4 3.1 %fusion.50 = bf16[16,256,258]{1,2,0:T(8,128)(2,1)} fusion(bf16[16,256,258]{1,2,0:T(8,128)(2,1)} %get-tuple-element.128, s32[]{:T(128)} %get-tuple-element.127, bf16[2048,258]{1,0:T(8,128)(2,1)} %get-tuple-element.138, s32[2048]{0:T(1024)S(1)} %broadcast_subtract_fusion.2, f32[256]{0:T(256)S(1)} %broadcast_maximum_fusion.2), kind=kOutput, calls=%fused_computation.8.clone.1 | convolution fusion | flops 271188992 | bytes 1717760 | tf_op jit(solution)/shard_map/while/body/eval_jaxpr/dot_general | solution.py:81
  102.0 3.1 %fusion.50 = bf16[16,256,258]{1,2,0:T(8,128)(2,1)} fusion(bf16[16,256,258]{1,2,0:T(8,128)(2,1)} %get-tuple-element.128, s32[]{:T(128)} %get-tuple-element.127, bf16[2048,258]{1,0:T(8,128)(2,1)} %get-tuple-element.138, s32[2048]{0:T(1024)S(1)} %broadcast_subtract_fusion.2, f32[256]{0:T(256)S(1)} %broadcast_maximum_fusion.2), kind=kOutput, calls=%fused_computation.8.clone.1 | convolution fusion | flops 271188992 | bytes 1717760 | tf_op jit(solution)/shard_map/while/body/eval_jaxpr/dot_general | solution.py:81
  106.7 3.0 %fusion.50 = bf16[16,256,258]{1,2,0:T(8,128)(2,1)} fusion(bf16[16,256,258]{1,2,0:T(8,128)(2,1)} %get-tuple-element.128, s32[]{:T(128)} %get-tuple-element.127, bf16[2048,258]{1,0:T(8,128)(2,1)} %get-tuple-element.138, s32[2048]{0:T(1024)S(1)} %broadcast_subtract_fusion.2, f32[256]{0:T(256)S(1)} %broadcast_maximum_fusion.2), kind=kOutput, calls=%fused_computation.8.clone.1 | convolution fusion | flops 271188992 | bytes 1717760 | tf_op jit(solution)/shard_map/while/body/eval_jaxpr/dot_general | solution.py:81
  111.4 3.1 %fusion.50 = bf16[16,256,258]{1,2,0:T(8,128)(2,1)} fusion(bf16[16,256,258]{1,2,0:T(8,128)(2,1)} %get-tuple-element.128, s32[]{:T(128)} %get-tuple-element.127, bf16[2048,258]{1,0:T(8,128)(2,1)} %get-tuple-element.138, s32[2048]{0:T(1024)S(1)} %broadcast_subtract_fusion.2, f32[256]{0:T(256)S(1)} %broadcast_maximum_fusion.2), kind=kOutput, calls=%fused_computation.8.clone.1 | convolution fusion | flops 271188992 | bytes 1717760 | tf_op jit(solution)/shard_map/while/body/eval_jaxpr/dot_general | solution.py:81
  116.1 3.0 %fusion.50 = bf16[16,256,258]{1,2,0:T(8,128)(2,1)} fusion(bf16[16,256,258]{1,2,0:T(8,128)(2,1)} %get-tuple-element.128, s32[]{:T(128)} %get-tuple-element.127, bf16[2048,258]{1,0:T(8,128)(2,1)} %get-tuple-element.138, s32[2048]{0:T(1024)S(1)} %broadcast_subtract_fusion.2, f32[256]{0:T(256)S(1)} %broadcast_maximum_fusion.2), kind=kOutput, calls=%fused_computation.8.clone.1 | convolution fusion | flops 271188992 | bytes 1717760 | tf_op jit(solution)/shard_map/while/body/eval_jaxpr/dot_general | solution.py:81
  120.7 3.1 %fusion.50 = bf16[16,256,258]{1,2,0:T(8,128)(2,1)} fusion(bf16[16,256,258]{1,2,0:T(8,128)(2,1)} %get-tuple-element.128, s32[]{:T(128)} %get-tuple-element.127, bf16[2048,258]{1,0:T(8,128)(2,1)} %get-tuple-element.138, s32[2048]{0:T(1024)S(1)} %broadcast_subtract_fusion.2, f32[256]{0:T(256)S(1)} %broadcast_maximum_fusion.2), kind=kOutput, calls=%fused_computation.8.clone.1 | convolution fusion | flops 271188992 | bytes 1717760 | tf_op jit(solution)/shard_map/while/body/eval_jaxpr/dot_general | solution.py:81
  125.4 3.0 %fusion.50 = bf16[16,256,258]{1,2,0:T(8,128)(2,1)} fusion(bf16[16,256,258]{1,2,0:T(8,128)(2,1)} %get-tuple-element.128, s32[]{:T(128)} %get-tuple-element.127, bf16[2048,258]{1,0:T(8,128)(2,1)} %get-tuple-element.138, s32[2048]{0:T(1024)S(1)} %broadcast_subtract_fusion.2, f32[256]{0:T(256)S(1)} %broadcast_maximum_fusion.2), kind=kOutput, calls=%fused_computation.8.clone.1 | convolution fusion | flops 271188992 | bytes 1717760 | tf_op jit(solution)/shard_map/while/body/eval_jaxpr/dot_general | solution.py:81
  130.0 3.1 %fusion.50 = bf16[16,256,258]{1,2,0:T(8,128)(2,1)} fusion(bf16[16,256,258]{1,2,0:T(8,128)(2,1)} %get-tuple-element.128, s32[]{:T(128)} %get-tuple-element.127, bf16[2048,258]{1,0:T(8,128)(2,1)} %get-tuple-element.138, s32[2048]{0:T(1024)S(1)} %broadcast_subtract_fusion.2, f32[256]{0:T(256)S(1)} %broadcast_maximum_fusion.2), kind=kOutput, calls=%fused_computation.8.clone.1 | convolution fusion | flops 271188992 | bytes 1717760 | tf_op jit(solution)/shard_map/while/body/eval_jaxpr/dot_general | solution.py:81
  134.7 3.1 %fusion.50 = bf16[16,256,258]{1,2,0:T(8,128)(2,1)} fusion(bf16[16,256,258]{1,2,0:T(8,128)(2,1)} %get-tuple-element.128, s32[]{:T(128)} %get-tuple-element.127, bf16[2048,258]{1,0:T(8,128)(2,1)} %get-tuple-element.138, s32[2048]{0:T(1024)S(1)} %broadcast_subtract_fusion.2, f32[256]{0:T(256)S(1)} %broadcast_maximum_fusion.2), kind=kOutput, calls=%fused_computation.8.clone.1 | convolution fusion | flops 271188992 | bytes 1717760 | tf_op jit(solution)/shard_map/while/body/eval_jaxpr/dot_general | solution.py:81
  139.4 3.0 %fusion.50 = bf16[16,256,258]{1,2,0:T(8,128)(2,1)} fusion(bf16[16,256,258]{1,2,0:T(8,128)(2,1)} %get-tuple-element.128, s32[]{:T(128)} %get-tuple-element.127, bf16[2048,258]{1,0:T(8,128)(2,1)} %get-tuple-element.138, s32[2048]{0:T(1024)S(1)} %broadcast_subtract_fusion.2, f32[256]{0:T(256)S(1)} %broadcast_maximum_fusion.2), kind=kOutput, calls=%fused_computation.8.clone.1 | convolution fusion | flops 271188992 | bytes 1717760 | tf_op jit(solution)/shard_map/while/body/eval_jaxpr/dot_general | solution.py:81
  144.0 3.1 %fusion.50 = bf16[16,256,258]{1,2,0:T(8,128)(2,1)} fusion(bf16[16,256,258]{1,2,0:T(8,128)(2,1)} %get-tuple-element.128, s32[]{:T(128)} %get-tuple-element.127, bf16[2048,258]{1,0:T(8,128)(2,1)} %get-tuple-element.138, s32[2048]{0:T(1024)S(1)} %broadcast_subtract_fusion.2, f32[256]{0:T(256)S(1)} %broadcast_maximum_fusion.2), kind=kOutput, calls=%fused_computation.8.clone.1 | convolution fusion | flops 271188992 | bytes 1717760 | tf_op jit(solution)/shard_map/while/body/eval_jaxpr/dot_general | solution.py:81
  148.7 3.1 %fusion.50 = bf16[16,256,258]{1,2,0:T(8,128)(2,1)} fusion(bf16[16,256,258]{1,2,0:T(8,128)(2,1)} %get-tuple-element.128, s32[]{:T(128)} %get-tuple-element.127, bf16[2048,258]{1,0:T(8,128)(2,1)} %get-tuple-element.138, s32[2048]{0:T(1024)S(1)} %broadcast_subtract_fusion.2, f32[256]{0:T(256)S(1)} %broadcast_maximum_fusion.2), kind=kOutput, calls=%fused_computation.8.clone.1 | convolution fusion | flops 271188992 | bytes 1717760 | tf_op jit(solution)/shard_map/while/body/eval_jaxpr/dot_general | solution.py:81
  151.7 2.1 copy.39
  153.8 74.1 %all-gather.2.cloned.1.call-done = bf16[129,2,256,128]{3,2,0,1:T(8,128)(2,1)} async-done(((bf16[129,2,16,128]{3,2,0,1:T(8,128)(2,1)}), bf16[129,2,256,128]{3,2,0,1:T(8,128)(2,1)}) %all-gather.2.cloned.1.call-update) | async-done | bytes 16908304 | tf_op jit(solution)/shard_map/all_gather | solution.py:120
  227.9 4.8 %fusion.12 = f32[129,16,128]{2,1,0:T(8,128)S(1)} fusion(bf16[129,2,256,128]{3,2,0,1:T(8,128)(2,1)} %all-gather.2.cloned.1.call-done, bf16[129,2,16,256]{3,2,0,1:T(8,128)(2,1)S(1)} %bitcast.76), kind=kOutput, calls=%fused_computation.18 | convolution fusion | flops 135266304 | bytes 10567680 | tf_op jit(solution)/shard_map/bhv,bvy->bhy/dot_general | solution.py:95
  232.7 5.4 %fusion.11 = f32[129,16,128]{2,1,0:T(8,128)S(1)} fusion(bf16[129,2,256,128]{3,2,0,1:T(8,128)(2,1)} %all-gather.2.cloned.1.call-done, bf16[129,2,16,256]{3,2,0,1:T(8,128)(2,1)S(1)} %bitcast.77), kind=kOutput, calls=%fused_computation.17 | convolution fusion | flops 135266304 | bytes 10567680 | tf_op jit(solution)/shard_map/bhv,bvy->bhy/dot_general | solution.py:95
  238.5 1.3 fusion.24
  241.4 13.3 %all_to_all.16 = bf16[2,129,2,8,128]{4,3,1,2,0:T(8,128)(2,1)S(1)} all-to-all(bf16[2,129,2,8,128]{4,3,1,2,0:T(8,128)(2,1)S(1)} %copy_bitcast_fusion), channel_id=1, replica_groups=mesh['shot'=16,'rcv'=8,'surf'=2] {'surf'}, dimensions={0} | all-to-all | bytes 2113536 | tf_op jit(solution)/shard_map/all_to_all | solution.py:18
  (98 shorter events, 22.0 us)
Async XLA Ops:
  6.5 3.0 %copy-start = (bf16[1,1024,256]{2,1,0:T(8,128)(2,1)S(1)}, bf16[1,1024,256]{2,1,0:T(8,128)(2,1)}, u32[]{:S(2)}) copy-start(bf16[1,1024,256]{2,1,0:T(8,128)(2,1)} %param.7) | copy-start | bytes 1572868
  6.5 221.4 %all-gather.2.cloned.1.call-start = ((), (), s32[]{:S(2)}) async-start(), calls=%async_computation.3 | async-start | bytes 17965056 | tf_op jit(solution)/shard_map/all_gather | solution.py:120
  10.3 0.7 copy-start.3
  13.7 11.9 %copy-start.4 = (s32[1,1024]{1,0:T(1,128)S(1)}, s32[1,1024]{1,0:T(1,128)}, u32[]{:S(2)}) copy-start(s32[1,1024]{1,0:T(1,128)} %param.10) | copy-start | bytes 12292
  13.7 11.9 %copy-start.5 = (s32[1,1024]{1,0:T(1,128)S(1)}, s32[1,1024]{1,0:T(1,128)}, u32[]{:S(2)}) copy-start(s32[1,1024]{1,0:T(1,128)} %param.9) | copy-start | bytes 12292
  15.5 47.1 %all-to-all-start.1 = ((bf16[16,128,2,129]{1,2,3,0:T(2,128)(2,1)}), bf16[16,128,2,129]{1,2,3,0:T(2,128)(2,1)S(1)}, u32[]{:S(2)}, u32[]{:S(2)}) async-start(bf16[16,128,2,129]{1,2,3,0:T(2,128)(2,1)} %copy.36), calls=%async_computation.1 | async-start | bytes 2113536 | tf_op jit(solution)/shard_map/all_to_all | solution.py:116
  62.6 4.4 %copy-start.2 = (bf16[16,128,2,129]{1,2,3,0:T(2,128)(2,1)}, bf16[16,128,2,129]{1,2,3,0:T(2,128)(2,1)S(1)}, u32[]{:S(2)}) copy-start(bf16[16,128,2,129]{1,2,3,0:T(2,128)(2,1)S(1)} %all-to-all-done.1) | copy-start | bytes 3170308
  62.6 14.5 %all-to-all-start = ((s32[16,1,128]{2,1,0:T(1,128)}), s32[16,1,128]{2,1,0:T(1,128)S(1)}, u32[]{:S(2)}, u32[]{:S(2)}) async-start(s32[16,1,128]{2,1,0:T(1,128)} %compare_select_fusion), calls=%async_computation | async-start | bytes 16384 | tf_op jit(solution)/shard_map/all_to_all | solution.py:117
  227.9 10.6 %copy-start.1 = (bf16[129,2,256,128]{3,2,0,1:T(8,128)(2,1)S(1)}, bf16[129,2,256,128]{3,2,0,1:T(8,128)(2,1)}, u32[]{:S(2)}) copy-start(bf16[129,2,256,128]{3,2,0,1:T(8,128)(2,1)} %all-gather.2.cloned.1.call-done) | copy-start | bytes 50724868
Sparse Core Ops, SparseCore 0:
  9.1 218.7 all-gather.1
where the time goes:
time: 265 us; the launch traced here: 263 us
  waiting for transfers between devices  109 us (41%)
  matrix products  64.6 us (24%)
  local copies, waits for them, and re-layouts  28.3 us (11%)
  starting transfers between devices  14.4 us (5%)
  between operations  13.6 us (5%)
  blocking collectives  13.3 us (5%)
  loops' own time  10.6 us (4%)
  other arithmetic  9.28 us (4%)
    all_gather x1, waiting for transfers between devices, local(): receiver = lax.all_gather(recv_panel, 'shot', axis=2, tiled=True)  74.1 us
    dot_general x16, matrix products, one_shot(): lax.dot_general(point_hit.astype(jnp.bfloat16), flat_rows, (((0,), (0,)),...  48.9 us
    all_to_all x1, waiting for transfers between devices, local(): lax.all_to_all(buffer, 'shot', split_axis=0, concat_axis=0, tiled=True)  34.8 us
    unnamed x17, local copies, waits for them, and re-layouts  13.9 us
    all_to_all x1, blocking collectives, summed_on_arrival(): parts = lax.all_to_all(split_up(array, dim, size), axis, 0, 0, tiled=True)  13.3 us
    dot_general x4, matrix products, product(): jnp.einsum('bhv,bvy->bhy', left_edge, right_edge, preferred_element_type=...  12.7 us
    another operation x1, loops' own time, bin_panel(): panel = lax.map(one_shot, jnp.arange(shot_rows, dtype=jnp.int32))  10.6 us
    all_to_all x1, starting transfers between devices, local(): lax.all_to_all(buffer, 'shot', split_axis=0, concat_axis=0, tiled=True)  10 us
  transfers between devices with their start and end apart: 3, of which 2 were waited for; matrix products, arithmetic and copies ran while one was open for 32% of the time, Pallas kernels for 0%

commit v1 on v0

v1 whole, which is shorter than its diff:
```python
import math

import jax
import jax.numpy as jnp
import numpy as np
from jax import lax
from jax.experimental import pallas as pl
from jax.experimental.pallas import tpu as pltpu
from jax.sharding import PartitionSpec as P

SHOTS = 16
SPAN = 8
PART = 128
PARTS = 8
CAP = 16
POINTS = 256
RCV = 128
F32 = jnp.float32
BF16 = jnp.bfloat16
NT = (((1,), (1,)), ((), ()))


def transform_table(window, freqs):
    phase = (np.arange(freqs)[:, None] * np.arange(window)[None, :] % window) * (2 * math.pi / window)
    table = np.zeros((2 * freqs + 6, window), np.float32)
    table[0 : 2 * freqs : 2] = np.cos(phase) / math.sqrt(window)
    table[1 : 2 * freqs : 2] = -np.sin(phase) / math.sqrt(window)
    high = table.astype(BF16)
    return high, (table - high.astype(np.float32)).astype(BF16)


def kernel(
    traces, block_ids, shot_ids, point_ids, table_high, table_low, recv, out,
    spec_out, spec_in, last_out, last_in, meta_out, meta_in, slots, extras, panel,
    points, part, other, final,
    spec_send, spec_recv, last_send, last_recv, meta_send, meta_recv,
    recv_send, recv_recv, swap_send, swap_recv, out_send, out_recv,
):
    me = lax.axis_index("shot")
    core = lax.axis_index("surf")
    column, ring = me // 8, me % 8

    def ahead(step):
        return (column + step % 2) % 2 * 8 + (ring + step // 2) % 8

    def behind(step):
        return (column + step % 2) % 2 * 8 + (ring + 8 - step // 2) % 8

    def remote(src, dst, send, arrive, **where):
        return pltpu.make_async_remote_copy(
            src_ref=src, dst_ref=dst, send_sem=send, recv_sem=arrive,
            device_id=where, device_id_type=pl.DeviceIdType.MESH,
        )

    last_in[...] = jnp.zeros_like(last_in)
    barrier = pltpu.get_barrier_semaphore()

    @pl.loop(1, SHOTS)
    def _(step):
        pl.semaphore_signal(
            barrier, inc=1, device_id={"shot": ahead(step)}, device_id_type=pl.DeviceIdType.MESH
        )

    pl.semaphore_signal(
        barrier, inc=1, device_id={"surf": 1 - core}, device_id_type=pl.DeviceIdType.MESH
    )

    samples = traces[0]
    spectra = lax.dot_general(table_high[...], samples, NT, preferred_element_type=F32)
    spectra += lax.dot_general(table_low[...], samples, NT, preferred_element_type=F32)
    spec_out[...] = spectra[:256].reshape(SHOTS, 16, 1024).astype(BF16)
    last_out[...] = spectra[256:258].astype(BF16)

    owners = block_ids[...]
    earlier = (
        lax.broadcasted_iota(jnp.int32, (PART, PART), 0)
        < lax.broadcasted_iota(jnp.int32, (PART, PART), 1)
    ).astype(F32).astype(BF16)
    for index in range(PARTS):
        lanes = slice(index * PART, (index + 1) * PART)
        owner = owners[:, lanes]
        hit = owner == lax.broadcasted_iota(jnp.int32, (SHOTS, PART), 0)
        before = jnp.dot(hit.astype(F32).astype(BF16), earlier, preferred_element_type=F32)
        rank = jnp.sum(jnp.where(hit, before, 0.0), axis=0, keepdims=True).astype(jnp.int32)
        place = rank + index * CAP
        meta_out[:, lanes] = (
            (owner * 128 + place) * 4096 + shot_ids[:, lanes] * 256 + point_ids[:, lanes]
        )

    pl.semaphore_wait(barrier, SHOTS)

    def send_spec(step):
        peer = ahead(step)
        return (
            remote(spec_out.at[peer], spec_in.at[me], spec_send.at[step], spec_recv.at[me], shot=peer),
            remote(meta_out, meta_in.at[me], meta_send.at[step], meta_recv.at[me], shot=peer),
        )

    def send_last():
        return remote(last_out, last_in.at[me], last_send.at[0], last_recv.at[me], shot=0)

    own_copies = (
        pltpu.make_async_copy(spec_out.at[me], spec_in.at[me], spec_recv.at[me]),
        pltpu.make_async_copy(meta_out, meta_in.at[me], meta_recv.at[me]),
    )
    own_last = pltpu.make_async_copy(last_out, last_in.at[me], last_recv.at[me])

    @pl.loop(1, SHOTS)
    def _(step):
        for copy in send_spec(step):
            copy.start()

    for copy in own_copies:
        copy.start()

    @pl.when(me == 0)
    def _():
        own_last.start()

    @pl.when(me != 0)
    def _():
        send_last().start()

    def rows_of(index):
        return pl.ds(pl.multiple_of(index * 16, 16), 16)

    def send_recv(freq, step):
        peer = ahead(step)
        return remote(
            recv.at[peer * SPAN + freq], points.at[freq, :, rows_of(me), :],
            recv_send.at[freq], recv_recv.at[freq], shot=peer,
        )

    def own_recv(source, freq):
        return pltpu.make_async_copy(
            recv.at[source], points.at[freq, :, rows_of(me), :], recv_recv.at[freq]
        )

    def send_recv_last():
        return remote(
            recv.at[SHOTS * SPAN], points.at[SPAN, :, rows_of(me), :],
            recv_send.at[SPAN], recv_recv.at[SPAN], shot=0,
        )

    @pl.loop(0, SPAN)
    def _(freq):
        own_recv(me * SPAN + freq, freq).start()

        @pl.loop(1, SHOTS)
        def _(step):
            send_recv(freq, step).start()

    @pl.when(me == 0)
    def _():
        own_recv(SHOTS * SPAN, SPAN).start()

    @pl.when(me != 0)
    def _():
        send_recv_last().start()

    @pl.loop(0, SHOTS)
    def _(step):
        source = behind(step)
        pltpu.make_async_copy(spec_in.at[source], spec_in.at[source], spec_recv.at[source]).wait()
        pltpu.make_async_copy(meta_in.at[source], meta_in.at[source], meta_recv.at[source]).wait()

        @pl.when(me == 0)
        def _():
            pltpu.make_async_copy(last_in.at[source], last_in.at[source], last_recv.at[source]).wait()

        meta = meta_in[source]
        owner = meta // (128 * 4096)
        place = meta // 4096 % 128
        shot = (meta // 256 % 16 + 1).astype(F32)
        point = (meta % 256).astype(F32)
        values = spec_in[source].astype(F32)
        final_values = last_in[source].astype(F32)
        hit = owner == lax.broadcasted_iota(jnp.int32, (SHOTS, 1024), 0)
        lines = [jnp.where(owner == block, values, 0.0).astype(BF16) for block in range(SHOTS)]
        for line in (final_values[0:1], final_values[1:2], shot, point):
            lines.append(jnp.where(hit, line, 0.0).astype(BF16))
        target = (place == lax.broadcasted_iota(jnp.int32, (PART, 1024), 0)).astype(F32).astype(BF16)
        routed = lax.dot_general(
            jnp.concatenate(lines, axis=0), target, NT, preferred_element_type=F32
        )
        lanes = pl.ds(pl.multiple_of(source * PART, PART), PART)
        slots[:, :, lanes] = routed[:256].reshape(SHOTS, 16, PART)
        extras[:, :, lanes] = routed[256:].reshape(4, SHOTS, PART)

    @pl.loop(0, SHOTS)
    def _(block):
        row = pl.ds(block, 1)
        shot_hit = extras[2, row, :] == (
            lax.broadcasted_iota(jnp.int32, (16, 2048), 0) + 1
        ).astype(F32)
        lines = [
            jnp.where(shot_hit, slots[block, line : line + 1, :], 0.0).astype(BF16)
            for line in range(16)
        ]
        lines += [jnp.where(shot_hit, extras[line, row, :], 0.0).astype(BF16) for line in (0, 1)]
        lines.append(shot_hit.astype(F32).astype(BF16))
        point_hit = (
            extras[3, row, :] == lax.broadcasted_iota(jnp.int32, (POINTS, 2048), 0).astype(F32)
        ).astype(F32).astype(BF16)
        sums = lax.dot_general(
            jnp.concatenate(lines, axis=0), point_hit, NT, preferred_element_type=F32
        )
        scale = 1.0 / jnp.maximum(sums[288:304], 1.0)
        panel[:, rows_of(block), :] = (
            sums[:288].reshape(18, 16, POINTS) * scale[None]
        ).astype(BF16)

    def swap(freq):
        return remote(
            part.at[freq, 1 - core], other.at[freq], swap_send.at[freq], swap_recv.at[freq],
            surf=1 - core,
        )

    def multiply(freq):
        pltpu.make_async_copy(points.at[freq], points.at[freq], recv_recv.at[freq]).wait()
        both = jnp.concatenate([points[freq, 0], points[freq, 1]], axis=1)
        shots = panel[pl.ds(2 * freq, 2)].reshape(512, POINTS)
        terms = jnp.dot(shots, both, preferred_element_type=F32)
        real = terms[:256, :RCV] - terms[256:, RCV:]
        imag = terms[:256, RCV:] + terms[256:, :RCV]
        for index, value in enumerate((real, imag)):
            split = value.reshape(SHOTS, 2, 8, RCV)
            for half in range(2):
                part[freq, half, index] = split[:, half].astype(BF16)
        swap(freq).start()

    def send_out(freq, step):
        peer = ahead(step)
        return remote(
            final.at[freq, :, peer], out.at[me * SPAN + freq], out_send.at[freq], out_recv.at[0],
            shot=peer,
        )

    def send_out_last(step):
        peer = ahead(step)
        return remote(
            final.at[SPAN, :, peer], out.at[SHOTS * SPAN], out_send.at[SPAN], out_recv.at[0],
            shot=peer,
        )

    def combine(freq):
        swap(freq).wait()
        total = part[freq, core].astype(F32) + other[freq].astype(F32)
        final[freq] = total.astype(BF16)

    def finish(freq):
        combine(freq)
        pltpu.make_async_copy(final.at[freq, :, me], out.at[me * SPAN + freq], out_recv.at[0]).start()

        @pl.loop(1, SHOTS)
        def _(step):
            send_out(freq, step).start()

    multiply(0)

    @pl.loop(1, SPAN)
    def _(freq):
        multiply(freq)
        finish(freq - 1)

    @pl.when(me == 0)
    def _():
        multiply(SPAN)

    finish(SPAN - 1)

    @pl.when(me == 0)
    def _():
        combine(SPAN)
        pltpu.make_async_copy(final.at[SPAN, :, me], out.at[SHOTS * SPAN], out_recv.at[0]).start()

        @pl.loop(1, SHOTS)
        def _(step):
            send_out_last(step).start()

        sent = final.at[SPAN, :, pl.ds(0, SHOTS - 1)]
        pltpu.make_async_copy(sent, sent, out_send.at[SPAN]).wait()

    @pl.loop(1, SHOTS)
    def _(step):
        for copy in send_spec(step):
            copy.wait_send()

    @pl.when(me != 0)
    def _():
        send_last().wait_send()
        send_recv_last().wait_send()

    @pl.loop(0, SPAN)
    def _(freq):
        sent = points.at[freq, :, pl.ds(0, 240), :]
        pltpu.make_async_copy(sent, sent, recv_send.at[freq]).wait()
        sent = final.at[freq, :, pl.ds(0, SHOTS - 1)]
        pltpu.make_async_copy(sent, sent, out_send.at[freq]).wait()

    pltpu.make_async_copy(out, out, out_recv.at[0]).wait()


def local(traces, trace_block, trace_shot, trace_point, recv_panel):
    rows, window = traces.shape[1:]
    freqs = recv_panel.shape[0]
    high, low = transform_table(window, freqs)
    vmem = pl.BlockSpec(memory_space=pltpu.VMEM)
    hbm = pl.BlockSpec(memory_space=pl.ANY)
    dma = pltpu.SemaphoreType.DMA
    return pl.pallas_call(
        kernel,
        out_shape=jax.ShapeDtypeStruct((freqs, 2, 8, RCV), BF16),
        in_specs=[vmem] * 6 + [hbm],
        out_specs=hbm,
        scratch_shapes=[
            pltpu.VMEM((SHOTS, 16, rows), BF16),
            pltpu.VMEM((SHOTS, 16, rows), BF16),
            pltpu.VMEM((2, rows), BF16),
            pltpu.VMEM((SHOTS, 2, rows), BF16),
            pltpu.VMEM((1, rows), jnp.int32),
            pltpu.VMEM((SHOTS, 1, rows), jnp.int32),
            pltpu.VMEM((SHOTS, 16, 2048), F32),
            pltpu.VMEM((4, SHOTS, 2048), F32),
            pltpu.VMEM((18, 256, POINTS), BF16),
            pltpu.VMEM((SPAN + 1, 2, POINTS, RCV), BF16),
            pltpu.VMEM((SPAN + 1, 2, 2, SHOTS, 8, RCV), BF16),
            pltpu.VMEM((SPAN + 1, 2, SHOTS, 8, RCV), BF16),
            pltpu.VMEM((SPAN + 1, 2, SHOTS, 8, RCV), BF16),
            dma((SHOTS,)), dma((SHOTS,)), dma((1,)), dma((SHOTS,)), dma((SHOTS,)), dma((SHOTS,)),
            dma((SPAN + 1,)), dma((SPAN + 1,)), dma((SPAN + 1,)), dma((SPAN + 1,)),
            dma((SPAN + 1,)), dma((1,)),
        ],
        compiler_params=pltpu.CompilerParams(collective_id=0, has_side_effects=True),
        name="multiples",
    )(
        traces, trace_block.reshape(1, rows), trace_shot, trace_point,
        jnp.asarray(high), jnp.asarray(low), recv_panel,
    )


def solution(mesh):
    in_specs = (
        P("surf", "shot", None),
        P("surf", "shot", None),
        P("surf", "shot"),
        P("surf", "shot"),
        P(None, None, ("shot", "surf"), "rcv"),
    )
    out_specs = P(None, None, ("shot", "surf"), "rcv")
    return jax.shard_map(local, mesh=mesh, in_specs=in_specs, out_specs=out_specs, check_vma=False)
```

time: 265 us -> 61.4 us (0.23)
  waiting for transfers between devices: 109 us -> 0 us
  matrix products: 64.6 us -> 0 us
  Pallas kernels: 0 us -> 59.3 us
  local copies, waits for them, and re-layouts: 28.3 us -> 1.87 us
  starting transfers between devices: 14.4 us -> 0 us
  between operations: 13.6 us -> 0.01 us
  blocking collectives: 13.3 us -> 0 us
  loops' own time: 10.6 us -> 0 us
  other arithmetic: 9.28 us -> 0 us
    all_gather x1 -> x0, waiting for transfers between devices: 74.1 us -> none  [local(): receiver = lax.all_gather(recv_panel, 'shot', axis=2, tiled=True)]
    dot_general x24 -> x0, matrix products: 64.6 us -> none  [the longest x16 48.9 us: one_shot(): lax.dot_general(point_hit.astype(jnp.bfloat16), flat_rows, (((0,), (0,)),...]
    pallas_call x0 -> x1, Pallas kernels: none -> 59.3 us  [local(): pl.pallas_call(kernel, out_shape=jax.ShapeDtypeStruct((freqs, 2, 8, RCV),...]
    all_to_all x2 -> x0, waiting for transfers between devices: 34.8 us -> none  [the longest x1 34.8 us: local(): lax.all_to_all(buffer, 'shot', split_axis=0, concat_axis=0, tiled=True)]
    all_to_all x2 -> x0, starting transfers between devices: 14.4 us -> none  [the longest x1 10 us: local(): lax.all_to_all(buffer, 'shot', split_axis=0, concat_axis=0, tiled=True)]
    all_to_all x1 -> x0, blocking collectives: 13.3 us -> none  [summed_on_arrival(): parts = lax.all_to_all(split_up(array, dim, size), axis, 0, 0, tiled=True)]
    unnamed x17 -> x1, local copies, waits for them, and re-layouts: 13.9 us -> 1.87 us
    another operation x1 -> x0, loops' own time: 10.6 us -> none  [bin_panel(): panel = lax.map(one_shot, jnp.arange(shot_rows, dtype=jnp.int32))]
  transfers between devices with their start and end apart: 3 -> 0, of which waited for: 2 -> 0; matrix products, arithmetic and copies ran while one was open for 32% -> 0% of each run, Pallas kernels for 0% -> 0%
where the time goes in v1:
time: 61.4 us; the launch traced here: 61.2 us
  Pallas kernels  59.3 us (97%)
  local copies, waits for them, and re-layouts  1.87 us (3%)
    pallas_call x1, Pallas kernels, local(): pl.pallas_call(kernel, out_shape=jax.ShapeDtypeStruct((freqs, 2, 8, RCV),...  59.3 us
    unnamed x1, local copies, waits for them, and re-layouts  1.87 us

profile of v1, /device:TPU:1, one launch (start us, length us, event | category | flops | bytes accessed | tf_op | source)
XLA Modules:
  0.0 61.2 jit_solution(12690673184990688155)
XLA Ops:
  0.0 59.3 %multiples.1 = bf16[129,2,8,128]{3,2,1,0:T(8,128)(2,1)} custom-call(bf16[1,1024,256]{2,1,0:T(8,128)(2,1)} %traces.1, s32[1,1024]{1,0:T(1,128)} %bitcast.1, s32[1,1024]{1,0:T(1,128)} %shot_ids.1, s32[1,1024]{1,0:T(1,128)} %point_ids.1, bf16[264,256]{1,0:T(8,128)(2,1)} %constant.4.clone.table_high, bf16[264,256]{1,0:T(8,128)(2,1)} %constant.5.clone.table_low, ...), custom_call_target="tpu_custom_call" | custom-call | tf_op jit(solution)/shard_map/multiples/pallas_call | solution.py:311
  59.3 1.9 %copy.9 = bf16[129,2,8,128]{3,2,1,0:T(8,128)(2,1)} copy(bf16[129,2,8,128]{3,2,1,0:T(8,128)(2,1)} %multiples.1) | data formatting | bytes 1056768

commit v2 on v1

--- a/solution.py
+++ b/solution.py
@@ -11,7 +11,8 @@
 SHOTS = 16
 SPAN = 8
 PART = 128
-PARTS = 8
+ROWS = 256
+QUARTERS = 4
 CAP = 16
 POINTS = 256
 RCV = 128
@@ -31,20 +32,23 @@
 
 def kernel(
     traces, block_ids, shot_ids, point_ids, table_high, table_low, recv, out,
-    spec_out, spec_in, last_out, last_in, meta_out, meta_in, slots, extras, panel,
-    points, part, other, final,
-    spec_send, spec_recv, last_send, last_recv, meta_send, meta_recv,
+    samples, high, low, ids, spec_out, spec_all, last_out, last_all, meta_out, meta_all,
+    slots, extras, panel, points, part, other, final,
+    load_sem, spec_send, spec_recv, last_send, last_recv, meta_send, meta_recv,
+    gather_send, gather_recv,
     recv_send, recv_recv, swap_send, swap_recv, out_send, out_recv,
 ):
     me = lax.axis_index("shot")
+    mine = lax.axis_index("rcv") // 2
+    side = lax.axis_index("rcv") % 2
     core = lax.axis_index("surf")
     column, ring = me // 8, me % 8
 
     def ahead(step):
         return (column + step % 2) % 2 * 8 + (ring + step // 2) % 8
 
-    def behind(step):
-        return (column + step % 2) % 2 * 8 + (ring + 8 - step // 2) % 8
+    def beside(step):
+        return (mine + step) % QUARTERS * 2 + side
 
     def remote(src, dst, send, arrive, **where):
         return pltpu.make_async_remote_copy(
@@ -52,70 +56,80 @@
             device_id=where, device_id_type=pl.DeviceIdType.MESH,
         )
 
-    last_in[...] = jnp.zeros_like(last_in)
+    lanes = pl.ds(pl.multiple_of(mine * ROWS, ROWS), ROWS)
+    loads = [
+        pltpu.make_async_copy(traces.at[0, lanes, :], samples, load_sem.at[0]),
+        pltpu.make_async_copy(table_high, high, load_sem.at[1]),
+        pltpu.make_async_copy(table_low, low, load_sem.at[2]),
+        pltpu.make_async_copy(block_ids.at[:, lanes], ids.at[0], load_sem.at[3]),
+        pltpu.make_async_copy(shot_ids.at[:, lanes], ids.at[1], load_sem.at[4]),
+        pltpu.make_async_copy(point_ids.at[:, lanes], ids.at[2], load_sem.at[5]),
+    ]
+    for load in loads:
+        load.start()
+
+    last_all[...] = jnp.zeros_like(last_all)
     barrier = pltpu.get_barrier_semaphore()
 
     @pl.loop(1, SHOTS)
     def _(step):
         pl.semaphore_signal(
             barrier, inc=1, device_id={"shot": ahead(step)}, device_id_type=pl.DeviceIdType.MESH
+        )
+
+    @pl.loop(1, QUARTERS)
+    def _(step):
+        pl.semaphore_signal(
+            barrier, inc=1, device_id={"rcv": beside(step)}, device_id_type=pl.DeviceIdType.MESH
         )
 
     pl.semaphore_signal(
         barrier, inc=1, device_id={"surf": 1 - core}, device_id_type=pl.DeviceIdType.MESH
     )
-
-    samples = traces[0]
-    spectra = lax.dot_general(table_high[...], samples, NT, preferred_element_type=F32)
-    spectra += lax.dot_general(table_low[...], samples, NT, preferred_element_type=F32)
-    spec_out[...] = spectra[:256].reshape(SHOTS, 16, 1024).astype(BF16)
+    for load in loads:
+        load.wait()
+
+    spectra = lax.dot_general(high[...], samples[...], NT, preferred_element_type=F32)
+    spectra += lax.dot_general(low[...], samples[...], NT, preferred_element_type=F32)
+    spec_out[...] = spectra[:256].reshape(SHOTS, 16, ROWS).astype(BF16)
     last_out[...] = spectra[256:258].astype(BF16)
 
-    owners = block_ids[...]
     earlier = (
         lax.broadcasted_iota(jnp.int32, (PART, PART), 0)
         < lax.broadcasted_iota(jnp.int32, (PART, PART), 1)
     ).astype(F32).astype(BF16)
-    for index in range(PARTS):
-        lanes = slice(index * PART, (index + 1) * PART)
-        owner = owners[:, lanes]
-        hit = owner == lax.broadcasted_iota(jnp.int32, (SHOTS, PART), 0)
-        before = jnp.dot(hit.astype(F32).astype(BF16), earlier, preferred_element_type=F32)
-        rank = jnp.sum(jnp.where(hit, before, 0.0), axis=0, keepdims=True).astype(jnp.int32)
-        place = rank + index * CAP
-        meta_out[:, lanes] = (
-            (owner * 128 + place) * 4096 + shot_ids[:, lanes] * 256 + point_ids[:, lanes]
-        )
-
-    pl.semaphore_wait(barrier, SHOTS)
+    for index in range(ROWS // PART):
+        half = slice(index * PART, (index + 1) * PART)
+        owner = ids[0, :, half]
+        hits = owner == lax.broadcasted_iota(jnp.int32, (SHOTS, PART), 0)
+        before = jnp.dot(hits.astype(F32).astype(BF16), earlier, preferred_element_type=F32)
+        rank = jnp.sum(jnp.where(hits, before, 0.0), axis=0, keepdims=True).astype(jnp.int32)
+        place = (me % 8 * 2 + index) * CAP + rank
+        meta_out[:, half] = (owner * 256 + place) * 4096 + ids[1, :, half] * 256 + ids[2, :, half]
+
+    pl.semaphore_wait(barrier, SHOTS - 1 + QUARTERS - 1 + 1)
 
     def send_spec(step):
         peer = ahead(step)
         return (
-            remote(spec_out.at[peer], spec_in.at[me], spec_send.at[step], spec_recv.at[me], shot=peer),
-            remote(meta_out, meta_in.at[me], meta_send.at[step], meta_recv.at[me], shot=peer),
+            remote(spec_out.at[peer], spec_all.at[mine, me], spec_send.at[step], spec_recv.at[0], shot=peer),
+            remote(meta_out, meta_all.at[mine, me], meta_send.at[step], meta_recv.at[0], shot=peer),
         )
 
     def send_last():
-        return remote(last_out, last_in.at[me], last_send.at[0], last_recv.at[me], shot=0)
-
-    own_copies = (
-        pltpu.make_async_copy(spec_out.at[me], spec_in.at[me], spec_recv.at[me]),
-        pltpu.make_async_copy(meta_out, meta_in.at[me], meta_recv.at[me]),
-    )
-    own_last = pltpu.make_async_copy(last_out, last_in.at[me], last_recv.at[me])
+        return remote(last_out, last_all.at[mine, me], last_send.at[0], last_recv.at[0], shot=0)
 
     @pl.loop(1, SHOTS)
     def _(step):
         for copy in send_spec(step):
             copy.start()
 
-    for copy in own_copies:
-        copy.start()
+    pltpu.make_async_copy(spec_out.at[me], spec_all.at[mine, me], spec_recv.at[0]).start()
+    pltpu.make_async_copy(meta_out, meta_all.at[mine, me], meta_recv.at[0]).start()
 
     @pl.when(me == 0)
     def _():
-        own_last.start()
+        pltpu.make_async_copy(last_out, last_all.at[mine, me], last_recv.at[0]).start()
 
     @pl.when(me != 0)
     def _():
@@ -158,49 +172,86 @@
     def _():
         send_recv_last().start()
 
-    @pl.loop(0, SHOTS)
-    def _(step):
-        source = behind(step)
-        pltpu.make_async_copy(spec_in.at[source], spec_in.at[source], spec_recv.at[source]).wait()
-        pltpu.make_async_copy(meta_in.at[source], meta_in.at[source], meta_recv.at[source]).wait()
+    def arrived(buffer, index, sem):
+        whole = buffer.at[index]
+        pltpu.make_async_copy(whole, whole, sem).wait()
+
+    def gather(kind, buffer, step):
+        return remote(
+            buffer.at[mine], buffer.at[mine], gather_send.at[kind, step], gather_recv.at[kind, step],
+            rcv=beside(step),
+        )
+
+    arrived(spec_all, mine, spec_recv.at[0])
+    arrived(meta_all, mine, meta_recv.at[0])
+
+    @pl.when(me == 0)
+    def _():
+        arrived(last_all, mine, last_recv.at[0])
+
+    @pl.loop(1, QUARTERS)
+    def _(step):
+        gather(0, spec_all, step).start()
+        gather(1, meta_all, step).start()
 
         @pl.when(me == 0)
         def _():
-            pltpu.make_async_copy(last_in.at[source], last_in.at[source], last_recv.at[source]).wait()
-
-        meta = meta_in[source]
-        owner = meta // (128 * 4096)
-        place = meta // 4096 % 128
+            gather(2, last_all, step).start()
+
+    def place_rows(index, group):
+        sources = [group * 8 + source for source in range(8)]
+        meta = jnp.concatenate([meta_all[index, source] for source in sources], axis=1)
+        values = jnp.concatenate([spec_all[index, source] for source in sources], axis=1)
+        final_values = jnp.concatenate([last_all[index, source] for source in sources], axis=1)
+        values, final_values = values.astype(F32), final_values.astype(F32)
+        owner = meta // (256 * 4096)
+        place = meta // 4096 % 256
         shot = (meta // 256 % 16 + 1).astype(F32)
         point = (meta % 256).astype(F32)
-        values = spec_in[source].astype(F32)
-        final_values = last_in[source].astype(F32)
-        hit = owner == lax.broadcasted_iota(jnp.int32, (SHOTS, 1024), 0)
+        hit = owner == lax.broadcasted_iota(jnp.int32, (SHOTS, 2048), 0)
         lines = [jnp.where(owner == block, values, 0.0).astype(BF16) for block in range(SHOTS)]
         for line in (final_values[0:1], final_values[1:2], shot, point):
             lines.append(jnp.where(hit, line, 0.0).astype(BF16))
-        target = (place == lax.broadcasted_iota(jnp.int32, (PART, 1024), 0)).astype(F32).astype(BF16)
+        target = (place == lax.broadcasted_iota(jnp.int32, (256, 2048), 0)).astype(F32).astype(BF16)
         routed = lax.dot_general(
             jnp.concatenate(lines, axis=0), target, NT, preferred_element_type=F32
         )
-        lanes = pl.ds(pl.multiple_of(source * PART, PART), PART)
-        slots[:, :, lanes] = routed[:256].reshape(SHOTS, 16, PART)
-        extras[:, :, lanes] = routed[256:].reshape(4, SHOTS, PART)
-
-    @pl.loop(0, SHOTS)
+        places = pl.ds(pl.multiple_of((index * 2 + group) * 256, 256), 256)
+        slots[:, :, places] = routed[:256].reshape(SHOTS, 16, 256)
+        extras[:, :, places] = routed[256:].reshape(4, SHOTS, 256)
+
+    @pl.loop(0, 2)
+    def _(group):
+        place_rows(mine, group)
+
+    @pl.loop(1, QUARTERS)
+    def _(step):
+        index = (mine + QUARTERS - step) % QUARTERS
+        arrived(spec_all, index, gather_recv.at[0, step])
+        arrived(meta_all, index, gather_recv.at[1, step])
+
+        @pl.when(me == 0)
+        def _():
+            arrived(last_all, index, gather_recv.at[2, step])
+
+        @pl.loop(0, 2)
+        def _(group):
+            place_rows(index, group)
+
+    @pl.loop(0, SHOTS, unroll=4)
     def _(block):
-        row = pl.ds(block, 1)
-        shot_hit = extras[2, row, :] == (
+        line_of = pl.ds(block, 1)
+        shot_hit = extras[2, line_of, :] == (
             lax.broadcasted_iota(jnp.int32, (16, 2048), 0) + 1
         ).astype(F32)
         lines = [
             jnp.where(shot_hit, slots[block, line : line + 1, :], 0.0).astype(BF16)
             for line in range(16)
         ]
-        lines += [jnp.where(shot_hit, extras[line, row, :], 0.0).astype(BF16) for line in (0, 1)]
+        lines += [jnp.where(shot_hit, extras[line, line_of, :], 0.0).astype(BF16) for line in (0, 1)]
         lines.append(shot_hit.astype(F32).astype(BF16))
         point_hit = (
-            extras[3, row, :] == lax.broadcasted_iota(jnp.int32, (POINTS, 2048), 0).astype(F32)
+            extras[3, line_of, :] == lax.broadcasted_iota(jnp.int32, (POINTS, 2048), 0).astype(F32)
         ).astype(F32).astype(BF16)
         sums = lax.dot_general(
             jnp.concatenate(lines, axis=0), point_hit, NT, preferred_element_type=F32
@@ -286,6 +337,15 @@
         for copy in send_spec(step):
             copy.wait_send()
 
+    @pl.loop(1, QUARTERS)
+    def _(step):
+        gather(0, spec_all, step).wait_send()
+        gather(1, meta_all, step).wait_send()
+
+        @pl.when(me == 0)
+        def _():
+            gather(2, last_all, step).wait_send()
+
     @pl.when(me != 0)
     def _():
         send_last().wait_send()
@@ -305,21 +365,24 @@
     rows, window = traces.shape[1:]
     freqs = recv_panel.shape[0]
     high, low = transform_table(window, freqs)
-    vmem = pl.BlockSpec(memory_space=pltpu.VMEM)
-    hbm = pl.BlockSpec(memory_space=pl.ANY)
+    hbm = pl.BlockSpec(memory_space=pltpu.HBM)
     dma = pltpu.SemaphoreType.DMA
     return pl.pallas_call(
         kernel,
         out_shape=jax.ShapeDtypeStruct((freqs, 2, 8, RCV), BF16),
-        in_specs=[vmem] * 6 + [hbm],
-        out_specs=hbm,
+        in_specs=[hbm] * 7,
+        out_specs=pl.BlockSpec(memory_space=pl.ANY),
         scratch_shapes=[
-            pltpu.VMEM((SHOTS, 16, rows), BF16),
-            pltpu.VMEM((SHOTS, 16, rows), BF16),
-            pltpu.VMEM((2, rows), BF16),
-            pltpu.VMEM((SHOTS, 2, rows), BF16),
-            pltpu.VMEM((1, rows), jnp.int32),
-            pltpu.VMEM((SHOTS, 1, rows), jnp.int32),
+            pltpu.VMEM((ROWS, window), BF16),
+            pltpu.VMEM(high.shape, BF16),
+            pltpu.VMEM(low.shape, BF16),
+            pltpu.VMEM((3, 1, ROWS), jnp.int32),
+            pltpu.VMEM((SHOTS, 16, ROWS), BF16),
+            pltpu.VMEM((QUARTERS, SHOTS, 16, ROWS), BF16),
+            pltpu.VMEM((2, ROWS), BF16),
+            pltpu.VMEM((QUARTERS, SHOTS, 2, ROWS), BF16),
+            pltpu.VMEM((1, ROWS), jnp.int32),
+            pltpu.VMEM((QUARTERS, SHOTS, 1, ROWS), jnp.int32),
             pltpu.VMEM((SHOTS, 16, 2048), F32),
             pltpu.VMEM((4, SHOTS, 2048), F32),
             pltpu.VMEM((18, 256, POINTS), BF16),
@@ -327,7 +390,8 @@
             pltpu.VMEM((SPAN + 1, 2, 2, SHOTS, 8, RCV), BF16),
             pltpu.VMEM((SPAN + 1, 2, SHOTS, 8, RCV), BF16),
             pltpu.VMEM((SPAN + 1, 2, SHOTS, 8, RCV), BF16),
-            dma((SHOTS,)), dma((SHOTS,)), dma((1,)), dma((SHOTS,)), dma((SHOTS,)), dma((SHOTS,)),
+            dma((6,)), dma((SHOTS,)), dma((1,)), dma((1,)), dma((1,)), dma((SHOTS,)), dma((1,)),
+            dma((3, QUARTERS)), dma((3, QUARTERS)),
             dma((SPAN + 1,)), dma((SPAN + 1,)), dma((SPAN + 1,)), dma((SPAN + 1,)),
             dma((SPAN + 1,)), dma((1,)),
         ],

time: 61.4 us -> 54.1 us (0.88)
  Pallas kernels: 59.3 us -> 52.1 us
    pallas_call x1, Pallas kernels: 59.3 us -> 52.1 us  [local(): pl.pallas_call(kernel, out_shape=jax.ShapeDtypeStruct((freqs, 2, 8, RCV),...]
where the time goes in v2:
time: 54.1 us; the launch traced here: 54 us
  Pallas kernels  52.1 us (96%)
  local copies, waits for them, and re-layouts  1.87 us (3%)
    pallas_call x1, Pallas kernels, local(): pl.pallas_call(kernel, out_shape=jax.ShapeDtypeStruct((freqs, 2, 8, RCV),...  52.1 us
    unnamed x1, local copies, waits for them, and re-layouts  1.87 us

profile of v2, /device:TPU:1, one launch (start us, length us, event | category | flops | bytes accessed | tf_op | source)
XLA Modules:
  0.0 54.0 jit_solution(18279320529026021302)
XLA Ops:
  0.0 52.1 %multiples.1 = bf16[129,2,8,128]{3,2,1,0:T(8,128)(2,1)} custom-call(bf16[1,1024,256]{2,1,0:T(8,128)(2,1)} %traces.1, s32[1,1024]{1,0:T(1,128)} %bitcast.1, s32[1,1024]{1,0:T(1,128)} %shot_ids.1, s32[1,1024]{1,0:T(1,128)} %point_ids.1, bf16[264,256]{1,0:T(8,128)(2,1)} %constant.4.clone.table_high, bf16[264,256]{1,0:T(8,128)(2,1)} %constant.5.clone.table_low, ...), custom_call_target="tpu_custom_call" | custom-call | tf_op jit(solution)/shard_map/multiples/pallas_call | solution.py:370
  52.1 1.9 %copy.9 = bf16[129,2,8,128]{3,2,1,0:T(8,128)(2,1)} copy(bf16[129,2,8,128]{3,2,1,0:T(8,128)(2,1)} %multiples.1) | data formatting | bytes 1056768

commit v3 on v2

--- a/solution.py
+++ b/solution.py
@@ -11,9 +11,9 @@
 SHOTS = 16
 SPAN = 8
 PART = 128
-ROWS = 256
-QUARTERS = 4
+PARTS = 8
 CAP = 16
+LAST = 15
 POINTS = 256
 RCV = 128
 F32 = jnp.float32
@@ -39,16 +39,28 @@
     recv_send, recv_recv, swap_send, swap_recv, out_send, out_recv,
 ):
     me = lax.axis_index("shot")
-    mine = lax.axis_index("rcv") // 2
-    side = lax.axis_index("rcv") % 2
+    mine = lax.axis_index("rcv")
+    row, side = mine // 2, mine % 2
     core = lax.axis_index("surf")
     column, ring = me // 8, me % 8
 
     def ahead(step):
         return (column + step % 2) % 2 * 8 + (ring + step // 2) % 8
 
+    def owned(index):
+        return (index // 8 + side) % 2 * 8 + index % 8
+
+    own = owned(me)
+    last_home = owned(LAST)
+
     def beside(step):
-        return (mine + step) % QUARTERS * 2 + side
+        return {
+            "shot": (column + step % 2) % 2 * 8 + ring,
+            "rcv": (row + step // 2) % 4 * 2 + (side + step % 2) % 2,
+        }
+
+    def beside_back(step):
+        return (row + 4 - step // 2) % 4 * 2 + (side + step % 2) % 2
 
     def remote(src, dst, send, arrive, **where):
         return pltpu.make_async_remote_copy(
@@ -56,7 +68,7 @@
             device_id=where, device_id_type=pl.DeviceIdType.MESH,
         )
 
-    lanes = pl.ds(pl.multiple_of(mine * ROWS, ROWS), ROWS)
+    lanes = pl.ds(pl.multiple_of(mine * PART, PART), PART)
     loads = [
         pltpu.make_async_copy(traces.at[0, lanes, :], samples, load_sem.at[0]),
         pltpu.make_async_copy(table_high, high, load_sem.at[1]),
@@ -77,10 +89,10 @@
             barrier, inc=1, device_id={"shot": ahead(step)}, device_id_type=pl.DeviceIdType.MESH
         )
 
-    @pl.loop(1, QUARTERS)
+    @pl.loop(1, PARTS)
     def _(step):
         pl.semaphore_signal(
-            barrier, inc=1, device_id={"rcv": beside(step)}, device_id_type=pl.DeviceIdType.MESH
+            barrier, inc=1, device_id=beside(step), device_id_type=pl.DeviceIdType.MESH
         )
 
     pl.semaphore_signal(
@@ -91,47 +103,44 @@
 
     spectra = lax.dot_general(high[...], samples[...], NT, preferred_element_type=F32)
     spectra += lax.dot_general(low[...], samples[...], NT, preferred_element_type=F32)
-    spec_out[...] = spectra[:256].reshape(SHOTS, 16, ROWS).astype(BF16)
+    spec_out[...] = spectra[:256].reshape(SHOTS, 16, PART).astype(BF16)
     last_out[...] = spectra[256:258].astype(BF16)
 
     earlier = (
         lax.broadcasted_iota(jnp.int32, (PART, PART), 0)
         < lax.broadcasted_iota(jnp.int32, (PART, PART), 1)
     ).astype(F32).astype(BF16)
-    for index in range(ROWS // PART):
-        half = slice(index * PART, (index + 1) * PART)
-        owner = ids[0, :, half]
-        hits = owner == lax.broadcasted_iota(jnp.int32, (SHOTS, PART), 0)
-        before = jnp.dot(hits.astype(F32).astype(BF16), earlier, preferred_element_type=F32)
-        rank = jnp.sum(jnp.where(hits, before, 0.0), axis=0, keepdims=True).astype(jnp.int32)
-        place = (me % 8 * 2 + index) * CAP + rank
-        meta_out[:, half] = (owner * 256 + place) * 4096 + ids[1, :, half] * 256 + ids[2, :, half]
-
-    pl.semaphore_wait(barrier, SHOTS - 1 + QUARTERS - 1 + 1)
+    owners = ids[0]
+    hits = owners == lax.broadcasted_iota(jnp.int32, (SHOTS, PART), 0)
+    before = jnp.dot(hits.astype(F32).astype(BF16), earlier, preferred_element_type=F32)
+    rank = jnp.sum(jnp.where(hits, before, 0.0), axis=0, keepdims=True).astype(jnp.int32)
+    meta_out[...] = (owners * 256 + me * CAP + rank) * 4096 + ids[1] * 256 + ids[2]
+
+    pl.semaphore_wait(barrier, SHOTS - 1 + PARTS - 1 + 1)
 
     def send_spec(step):
         peer = ahead(step)
         return (
-            remote(spec_out.at[peer], spec_all.at[mine, me], spec_send.at[step], spec_recv.at[0], shot=peer),
+            remote(spec_out.at[owned(peer)], spec_all.at[mine, me], spec_send.at[step], spec_recv.at[0], shot=peer),
             remote(meta_out, meta_all.at[mine, me], meta_send.at[step], meta_recv.at[0], shot=peer),
         )
 
     def send_last():
-        return remote(last_out, last_all.at[mine, me], last_send.at[0], last_recv.at[0], shot=0)
+        return remote(last_out, last_all.at[mine, me], last_send.at[0], last_recv.at[0], shot=last_home)
 
     @pl.loop(1, SHOTS)
     def _(step):
         for copy in send_spec(step):
             copy.start()
 
-    pltpu.make_async_copy(spec_out.at[me], spec_all.at[mine, me], spec_recv.at[0]).start()
+    pltpu.make_async_copy(spec_out.at[own], spec_all.at[mine, me], spec_recv.at[0]).start()
     pltpu.make_async_copy(meta_out, meta_all.at[mine, me], meta_recv.at[0]).start()
 
-    @pl.when(me == 0)
+    @pl.when(own == LAST)
     def _():
         pltpu.make_async_copy(last_out, last_all.at[mine, me], last_recv.at[0]).start()
 
-    @pl.when(me != 0)
+    @pl.when(own != LAST)
     def _():
         send_last().start()
 
@@ -141,7 +150,7 @@
     def send_recv(freq, step):
         peer = ahead(step)
         return remote(
-            recv.at[peer * SPAN + freq], points.at[freq, :, rows_of(me), :],
+            recv.at[owned(peer) * SPAN + freq], points.at[freq, :, rows_of(me), :],
             recv_send.at[freq], recv_recv.at[freq], shot=peer,
         )
 
@@ -153,25 +162,25 @@
     def send_recv_last():
         return remote(
             recv.at[SHOTS * SPAN], points.at[SPAN, :, rows_of(me), :],
-            recv_send.at[SPAN], recv_recv.at[SPAN], shot=0,
-        )
+            recv_send.at[SPAN], recv_recv.at[SPAN], shot=last_home,
+        )
+
+    @pl.when(own == LAST)
+    def _():
+        own_recv(SHOTS * SPAN, SPAN).start()
+
+    @pl.when(own != LAST)
+    def _():
+        send_recv_last().start()
 
     @pl.loop(0, SPAN)
     def _(freq):
-        own_recv(me * SPAN + freq, freq).start()
+        own_recv(own * SPAN + freq, freq).start()
 
         @pl.loop(1, SHOTS)
         def _(step):
             send_recv(freq, step).start()
 
-    @pl.when(me == 0)
-    def _():
-        own_recv(SHOTS * SPAN, SPAN).start()
-
-    @pl.when(me != 0)
-    def _():
-        send_recv_last().start()
-
     def arrived(buffer, index, sem):
         whole = buffer.at[index]
         pltpu.make_async_copy(whole, whole, sem).wait()
@@ -179,30 +188,29 @@
     def gather(kind, buffer, step):
         return remote(
             buffer.at[mine], buffer.at[mine], gather_send.at[kind, step], gather_recv.at[kind, step],
-            rcv=beside(step),
+            **beside(step),
         )
 
     arrived(spec_all, mine, spec_recv.at[0])
     arrived(meta_all, mine, meta_recv.at[0])
 
-    @pl.when(me == 0)
+    @pl.when(own == LAST)
     def _():
         arrived(last_all, mine, last_recv.at[0])
 
-    @pl.loop(1, QUARTERS)
+    @pl.loop(1, PARTS)
     def _(step):
         gather(0, spec_all, step).start()
         gather(1, meta_all, step).start()
 
-        @pl.when(me == 0)
+        @pl.when(own == LAST)
         def _():
             gather(2, last_all, step).start()
 
-    def place_rows(index, group):
-        sources = [group * 8 + source for source in range(8)]
-        meta = jnp.concatenate([meta_all[index, source] for source in sources], axis=1)
-        values = jnp.concatenate([spec_all[index, source] for source in sources], axis=1)
-        final_values = jnp.concatenate([last_all[index, source] for source in sources], axis=1)
+    def place_rows(index):
+        meta = jnp.concatenate([meta_all[index, source] for source in range(SHOTS)], axis=1)
+        values = jnp.concatenate([spec_all[index, source] for source in range(SHOTS)], axis=1)
+        final_values = jnp.concatenate([last_all[index, source] for source in range(SHOTS)], axis=1)
         values, final_values = values.astype(F32), final_values.astype(F32)
         owner = meta // (256 * 4096)
         place = meta // 4096 % 256
@@ -216,29 +224,25 @@
         routed = lax.dot_general(
             jnp.concatenate(lines, axis=0), target, NT, preferred_element_type=F32
         )
-        places = pl.ds(pl.multiple_of((index * 2 + group) * 256, 256), 256)
+        places = pl.ds(pl.multiple_of(index * 256, 256), 256)
         slots[:, :, places] = routed[:256].reshape(SHOTS, 16, 256)
         extras[:, :, places] = routed[256:].reshape(4, SHOTS, 256)
 
-    @pl.loop(0, 2)
-    def _(group):
-        place_rows(mine, group)
-
-    @pl.loop(1, QUARTERS)
-    def _(step):
-        index = (mine + QUARTERS - step) % QUARTERS
+    place_rows(mine)
+
+    @pl.loop(1, PARTS)
+    def _(step):
+        index = beside_back(step)
         arrived(spec_all, index, gather_recv.at[0, step])
         arrived(meta_all, index, gather_recv.at[1, step])
 
-        @pl.when(me == 0)
+        @pl.when(own == LAST)
         def _():
             arrived(last_all, index, gather_recv.at[2, step])
 
-        @pl.loop(0, 2)
-        def _(group):
-            place_rows(index, group)
-
-    @pl.loop(0, SHOTS, unroll=4)
+        place_rows(index)
+
+    @pl.loop(0, SHOTS, unroll=8)
     def _(block):
         line_of = pl.ds(block, 1)
         shot_hit = extras[2, line_of, :] == (
@@ -283,7 +287,7 @@
     def send_out(freq, step):
         peer = ahead(step)
         return remote(
-            final.at[freq, :, peer], out.at[me * SPAN + freq], out_send.at[freq], out_recv.at[0],
+            final.at[freq, :, peer], out.at[own * SPAN + freq], out_send.at[freq], out_recv.at[0],
             shot=peer,
         )
 
@@ -301,52 +305,49 @@
 
     def finish(freq):
         combine(freq)
-        pltpu.make_async_copy(final.at[freq, :, me], out.at[me * SPAN + freq], out_recv.at[0]).start()
+        pltpu.make_async_copy(final.at[freq, :, me], out.at[own * SPAN + freq], out_recv.at[0]).start()
 
         @pl.loop(1, SHOTS)
         def _(step):
             send_out(freq, step).start()
 
+    @pl.when(own == LAST)
+    def _():
+        multiply(SPAN)
+
     multiply(0)
+
+    @pl.when(own == LAST)
+    def _():
+        combine(SPAN)
+        pltpu.make_async_copy(final.at[SPAN, :, me], out.at[SHOTS * SPAN], out_recv.at[0]).start()
+
+        @pl.loop(1, SHOTS)
+        def _(step):
+            send_out_last(step).start()
 
     @pl.loop(1, SPAN)
     def _(freq):
         multiply(freq)
         finish(freq - 1)
 
-    @pl.when(me == 0)
-    def _():
-        multiply(SPAN)
-
     finish(SPAN - 1)
-
-    @pl.when(me == 0)
-    def _():
-        combine(SPAN)
-        pltpu.make_async_copy(final.at[SPAN, :, me], out.at[SHOTS * SPAN], out_recv.at[0]).start()
-
-        @pl.loop(1, SHOTS)
-        def _(step):
-            send_out_last(step).start()
-
-        sent = final.at[SPAN, :, pl.ds(0, SHOTS - 1)]
-        pltpu.make_async_copy(sent, sent, out_send.at[SPAN]).wait()
 
     @pl.loop(1, SHOTS)
     def _(step):
         for copy in send_spec(step):
             copy.wait_send()
 
-    @pl.loop(1, QUARTERS)
+    @pl.loop(1, PARTS)
     def _(step):
         gather(0, spec_all, step).wait_send()
         gather(1, meta_all, step).wait_send()
 
-        @pl.when(me == 0)
+        @pl.when(own == LAST)
         def _():
             gather(2, last_all, step).wait_send()
 
-    @pl.when(me != 0)
+    @pl.when(own != LAST)
     def _():
         send_last().wait_send()
         send_recv_last().wait_send()
@@ -357,6 +358,11 @@
         pltpu.make_async_copy(sent, sent, recv_send.at[freq]).wait()
         sent = final.at[freq, :, pl.ds(0, SHOTS - 1)]
         pltpu.make_async_copy(sent, sent, out_send.at[freq]).wait()
+
+    @pl.when(own == LAST)
+    def _():
+        sent = final.at[SPAN, :, pl.ds(0, SHOTS - 1)]
+        pltpu.make_async_copy(sent, sent, out_send.at[SPAN]).wait()
 
     pltpu.make_async_copy(out, out, out_recv.at[0]).wait()
 
@@ -373,16 +379,16 @@
         in_specs=[hbm] * 7,
         out_specs=pl.BlockSpec(memory_space=pl.ANY),
         scratch_shapes=[
-            pltpu.VMEM((ROWS, window), BF16),
+            pltpu.VMEM((PART, window), BF16),
             pltpu.VMEM(high.shape, BF16),
             pltpu.VMEM(low.shape, BF16),
-            pltpu.VMEM((3, 1, ROWS), jnp.int32),
-            pltpu.VMEM((SHOTS, 16, ROWS), BF16),
-            pltpu.VMEM((QUARTERS, SHOTS, 16, ROWS), BF16),
-            pltpu.VMEM((2, ROWS), BF16),
-            pltpu.VMEM((QUARTERS, SHOTS, 2, ROWS), BF16),
-            pltpu.VMEM((1, ROWS), jnp.int32),
-            pltpu.VMEM((QUARTERS, SHOTS, 1, ROWS), jnp.int32),
+            pltpu.VMEM((3, 1, PART), jnp.int32),
+            pltpu.VMEM((SHOTS, 16, PART), BF16),
+            pltpu.VMEM((PARTS, SHOTS, 16, PART), BF16),
+            pltpu.VMEM((2, PART), BF16),
+            pltpu.VMEM((PARTS, SHOTS, 2, PART), BF16),
+            pltpu.VMEM((1, PART), jnp.int32),
+            pltpu.VMEM((PARTS, SHOTS, 1, PART), jnp.int32),
             pltpu.VMEM((SHOTS, 16, 2048), F32),
             pltpu.VMEM((4, SHOTS, 2048), F32),
             pltpu.VMEM((18, 256, POINTS), BF16),
@@ -391,15 +397,20 @@
             pltpu.VMEM((SPAN + 1, 2, SHOTS, 8, RCV), BF16),
             pltpu.VMEM((SPAN + 1, 2, SHOTS, 8, RCV), BF16),
             dma((6,)), dma((SHOTS,)), dma((1,)), dma((1,)), dma((1,)), dma((SHOTS,)), dma((1,)),
-            dma((3, QUARTERS)), dma((3, QUARTERS)),
+            dma((3, PARTS)), dma((3, PARTS)),
             dma((SPAN + 1,)), dma((SPAN + 1,)), dma((SPAN + 1,)), dma((SPAN + 1,)),
             dma((SPAN + 1,)), dma((1,)),
         ],
-        compiler_params=pltpu.CompilerParams(collective_id=0, has_side_effects=True),
+        compiler_params=pltpu.CompilerParams(collective_id=0, has_side_effects=True, vmem_limit_bytes=48 * 1024 * 1024),
         name="multiples",
     )(
-        traces, trace_block.reshape(1, rows), trace_shot, trace_point,
-        jnp.asarray(high), jnp.asarray(low), recv_panel,
+        *(
+            pltpu.with_memory_space_constraint(array, pltpu.HBM)
+            for array in (
+                traces, trace_block.reshape(1, rows), trace_shot, trace_point,
+                jnp.asarray(high), jnp.asarray(low), recv_panel,
+            )
+        )
     )
 
 

time: 54.1 us -> 51.9 us (0.959)
  Pallas kernels: 52.1 us -> 51 us
  local copies, waits for them, and re-layouts: 1.87 us -> 0.8 us
    pallas_call x1, Pallas kernels: 52.1 us -> 51 us  [local(): pl.pallas_call(kernel, out_shape=jax.ShapeDtypeStruct((freqs, 2, 8, RCV),...]
    unnamed x1, local copies, waits for them, and re-layouts: 1.87 us -> 0.8 us
where the time goes in v3:
time: 51.9 us; the launch traced here: 51.8 us
  Pallas kernels  51 us (98%)
  local copies, waits for them, and re-layouts  0.8 us (2%)
    pallas_call x1, Pallas kernels, local(): pl.pallas_call(kernel, out_shape=jax.ShapeDtypeStruct((freqs, 2, 8, RCV),...  51 us

profile of v3, /device:TPU:1, one launch (start us, length us, event | category | flops | bytes accessed | tf_op | source)
XLA Modules:
  0.0 51.8 jit_solution(13863190366268364788)
XLA Ops:
  0.0 51.0 %multiples.1 = bf16[129,2,8,128]{3,2,1,0:T(8,128)(2,1)S(1)} custom-call(bf16[1,1024,256]{2,1,0:T(8,128)(2,1)} %traces.1, s32[1,1024]{1,0:T(1,128)} %bitcast.1, s32[1,1024]{1,0:T(1,128)} %shot_ids.1, s32[1,1024]{1,0:T(1,128)} %point_ids.1, bf16[264,256]{1,0:T(8,128)(2,1)} %constant.4.clone.table_high, bf16[264,256]{1,0:T(8,128)(2,1)} %constant.5.clone.table_low, ...), custom_call_target="tpu_custom_call" | custom-call | tf_op jit(solution)/shard_map/multiples/pallas_call | solution.py:376
  51.0 0.8 %copy.9 = bf16[129,2,8,128]{3,2,1,0:T(8,128)(2,1)} copy(bf16[129,2,8,128]{3,2,1,0:T(8,128)(2,1)S(1)} %multiples.1) | data formatting | bytes 1056768

commit v4 on v3

--- a/solution.py
+++ b/solution.py
@@ -13,6 +13,8 @@
 PART = 128
 PARTS = 8
 CAP = 16
+FIRST = 3
+DEFER = 4
 LAST = 15
 POINTS = 256
 RCV = 128
@@ -309,7 +311,9 @@
 
         @pl.loop(1, SHOTS)
         def _(step):
-            send_out(freq, step).start()
+            @pl.when((freq < DEFER) | (ahead(step) % 8 < FIRST))
+            def _():
+                send_out(freq, step).start()
 
     @pl.when(own == LAST)
     def _():
@@ -332,6 +336,14 @@
         finish(freq - 1)
 
     finish(SPAN - 1)
+
+    @pl.loop(DEFER, SPAN)
+    def _(freq):
+        @pl.loop(1, SHOTS)
+        def _(step):
+            @pl.when(ahead(step) % 8 >= FIRST)
+            def _():
+                send_out(freq, step).start()
 
     @pl.loop(1, SHOTS)
     def _(step):

time: 51.9 us -> 51.6 us (level)
  no operation moved by 1% of the time
where the time goes in v4:
time: 51.6 us; the launch traced here: 51.5 us
  Pallas kernels  50.7 us (98%)
  local copies, waits for them, and re-layouts  0.8 us (2%)
    pallas_call x1, Pallas kernels, local(): pl.pallas_call(kernel, out_shape=jax.ShapeDtypeStruct((freqs, 2, 8, RCV),...  50.7 us

profile of v4, /device:TPU:1, one launch (start us, length us, event | category | flops | bytes accessed | tf_op | source)
XLA Modules:
  0.0 51.5 jit_solution(17239097635979254774)
XLA Ops:
  0.0 50.7 %multiples.1 = bf16[129,2,8,128]{3,2,1,0:T(8,128)(2,1)S(1)} custom-call(bf16[1,1024,256]{2,1,0:T(8,128)(2,1)} %traces.1, s32[1,1024]{1,0:T(1,128)} %bitcast.1, s32[1,1024]{1,0:T(1,128)} %shot_ids.1, s32[1,1024]{1,0:T(1,128)} %point_ids.1, bf16[264,256]{1,0:T(8,128)(2,1)} %constant.4.clone.table_high, bf16[264,256]{1,0:T(8,128)(2,1)} %constant.5.clone.table_low, ...), custom_call_target="tpu_custom_call" | custom-call | tf_op jit(solution)/shard_map/multiples/pallas_call | solution.py:388
  50.7 0.8 %copy.9 = bf16[129,2,8,128]{3,2,1,0:T(8,128)(2,1)} copy(bf16[129,2,8,128]{3,2,1,0:T(8,128)(2,1)S(1)} %multiples.1) | data formatting | bytes 1056768

commit v5 on v4

--- a/solution.py
+++ b/solution.py
@@ -82,7 +82,6 @@
     for load in loads:
         load.start()
 
-    last_all[...] = jnp.zeros_like(last_all)
     barrier = pltpu.get_barrier_semaphore()
 
     @pl.loop(1, SHOTS)
@@ -100,6 +99,11 @@
     pl.semaphore_signal(
         barrier, inc=1, device_id={"surf": 1 - core}, device_id_type=pl.DeviceIdType.MESH
     )
+
+    @pl.when(own != LAST)
+    def _():
+        last_all[...] = jnp.zeros_like(last_all)
+
     for load in loads:
         load.wait()
 

time: 51.6 us -> 51.3 us (level)
  no operation moved by 1% of the time
where the time goes in v5:
time: 51.3 us; the launch traced here: 51.2 us
  Pallas kernels  50.4 us (98%)
  local copies, waits for them, and re-layouts  0.8 us (2%)
    pallas_call x1, Pallas kernels, local(): pl.pallas_call(kernel, out_shape=jax.ShapeDtypeStruct((freqs, 2, 8, RCV),...  50.4 us

profile of v5, /device:TPU:1, one launch (start us, length us, event | category | flops | bytes accessed | tf_op | source)
XLA Modules:
  0.0 51.2 jit_solution(11235758988203500267)
XLA Ops:
  0.0 50.4 %multiples.1 = bf16[129,2,8,128]{3,2,1,0:T(8,128)(2,1)S(1)} custom-call(bf16[1,1024,256]{2,1,0:T(8,128)(2,1)} %traces.1, s32[1,1024]{1,0:T(1,128)} %bitcast.1, s32[1,1024]{1,0:T(1,128)} %shot_ids.1, s32[1,1024]{1,0:T(1,128)} %point_ids.1, bf16[264,256]{1,0:T(8,128)(2,1)} %constant.4.clone.table_high, bf16[264,256]{1,0:T(8,128)(2,1)} %constant.5.clone.table_low, ...), custom_call_target="tpu_custom_call" | custom-call | tf_op jit(solution)/shard_map/multiples/pallas_call | solution.py:392
  50.4 0.8 %copy.9 = bf16[129,2,8,128]{3,2,1,0:T(8,128)(2,1)} copy(bf16[129,2,8,128]{3,2,1,0:T(8,128)(2,1)S(1)} %multiples.1) | data formatting | bytes 1056768
